TPU v7x, 32 devices: a whole 2x2x4 slice. The times are simulated.
32 devices in a mesh: field: 4 (over z), vrow: 2 (over core), vcol: 4 (over y, x).
Axes of the slice: x: 2, y: 2, z: 4, core: 2. Of those that a mesh axis runs over, the one named last changes fastest.
Arguments:
- blocks: bfloat16 [1024, 24, 2, 256], P(('vrow', 'vcol'), 'field'), may hold values from 0 to 1
- block_ids: int32 [8, 4, 6], P(('vrow', 'vcol'), 'field'), may hold values from 0 to 11, as said below
- block_counts: int32 [8, 4], P(('vrow', 'vcol'), 'field'), may hold values from 1 to 6, as said below
Outputs:
- tables: float32 [1024, 2, 2, 4, 2, 128], P(('vrow', 'field'), None, None, 'vcol')
Inputs may be any that keep to these rules, and one draw needn't show every extreme that they name: `block_ids`: within each row of the last dimension the entries are distinct. `block_counts`: 6 is reached in every draw.
All inputs are finite; a program needn't handle non-finite values.
Results may differ from a plain program's by a relative error of at most 0.0003.
Values may be sent and summed in bfloat16 or wider, within the bound.
A program may use at most 64 MiB of HBM per device.

v0:
```python
import functools

import jax
import jax.numpy as jnp
from jax import lax
from jax.experimental import pallas as pl
from jax.experimental.pallas import tpu as pltpu
from jax.sharding import PartitionSpec as P

SBLK = 12
BLOCK = 256
MAX_PIECES = 4
MESH = pl.DeviceIdType.MESH


def partner(q, d, n):
    if n == 4:
        return (q + 1 - 2 * lax.rem(q, 2), lax.rem(q + 2, 4), 3 - q)[d - 1]
    return lax.rem(q + d, n)


def kernel(
    dims, scale, data, meta, out, rows, cols, part, got, rmeta, cmeta, rids, cids,
    col_local, row_local, meta_local,
    row_send, row_recv, col_send, col_recv, rm_send, rm_recv, cm_send, cm_recv,
    part_send, part_recv,
):
    n_field, n_vrow, n_vcol, pieces, occ, width, per_chunk = dims
    f, r, q = lax.axis_index("field"), lax.axis_index("vrow"), lax.axis_index("vcol")
    relay = n_vcol == 4

    barrier = pltpu.get_barrier_semaphore()
    for d in range(1, n_vcol):
        pl.semaphore_signal(barrier, inc=1, device_id={"vcol": partner(q, d, n_vcol)}, device_id_type=MESH)
    for d in range(1, n_vrow):
        pl.semaphore_signal(barrier, inc=1, device_id={"vrow": lax.rem(r + d, n_vrow)}, device_id_type=MESH)
    for d in range(1, n_field):
        pl.semaphore_signal(barrier, inc=1, device_id={"field": lax.rem(f + d, n_field)}, device_id_type=MESH)

    local = []
    for p in range(pieces):
        own = pltpu.make_async_copy(
            data.at[p], cols.at[0, pl.ds(0, occ), :, pl.ds(p * width, width), :], col_local.at[p]
        )
        own.start()
        local.append(own)
        own = pltpu.make_async_copy(data.at[p], rows.at[0, p], row_local.at[p])
        own.start()
        local.append(own)
    own_r = pltpu.make_async_copy(meta, rids.at[0], meta_local.at[0])
    own_r.start()
    own_c = pltpu.make_async_copy(meta, cids.at[0], meta_local.at[1])
    own_c.start()
    for v in range(n_vrow):
        cols[v, occ] = jnp.zeros_like(cols[v, occ])

    pl.semaphore_wait(barrier, n_vcol + n_vrow + n_field - 3)

    sends = []

    def send(src, dst, s, w, where):
        c = pltpu.make_async_remote_copy(
            src_ref=src, dst_ref=dst, send_sem=s, recv_sem=w, device_id=where, device_id_type=MESH
        )
        c.start()
        sends.append(c)
        return c

    row_meta, col_meta, row_copy, col_copy = {}, {}, {}, {}
    for d in range(1, n_vrow):
        to = {"vrow": lax.rem(r + d, n_vrow)}
        col_meta[d] = send(meta, cmeta.at[d], cm_send.at[d], cm_recv.at[d], to)
    for d in range(1, n_vcol):
        to = {"vcol": partner(q, d, n_vcol)}
        row_meta[d] = send(meta, rmeta.at[d], rm_send.at[d], rm_recv.at[d], to)
    for p in range(pieces):
        for d in range(1, n_vrow):
            to = {"vrow": lax.rem(r + d, n_vrow)}
            col_copy[d, p] = send(
                data.at[p],
                cols.at[d, pl.ds(0, occ), :, pl.ds(p * width, width), :],
                col_send.at[d, p], col_recv.at[d, p], to,
            )
        for d in range(1, 3 if relay else n_vcol):
            to = {"vcol": partner(q, d, n_vcol)}
            row_copy[d, p] = send(data.at[p], rows.at[d, p], row_send.at[d, p], row_recv.at[d, p], to)

    for c in local:
        c.wait()
    own_r.wait()
    own_c.wait()
    for d in range(1, n_vrow):
        col_meta[d].wait_recv()
        c = pltpu.make_async_copy(cmeta.at[d], cids.at[d], meta_local.at[1])
        c.start()
        c.wait()
    for d in range(1, n_vrow):
        for p in range(pieces):
            col_copy[d, p].wait_recv()

    half = occ // 2
    match = {}
    part_sends = []

    def matches(d):
        if d:
            row_meta[d].wait_recv()
            c = pltpu.make_async_copy(rmeta.at[d], rids.at[d], meta_local.at[0])
            c.start()
            c.wait()
        theirs = [[cids[v, 0, o] for o in range(occ)] for v in range(n_vrow)]
        found = []
        for o in range(occ):
            mine = rids[d, 0, o]
            for v in range(n_vrow):
                m = jnp.int32(occ)
                for k in range(occ):
                    m = jnp.where((mine >= 0) & (mine == theirs[v][k]), jnp.int32(k), m)
                found.append(m)
        return found

    def compute(d, p):
        if d not in match:
            match[d] = matches(d)
        for v in range(n_vrow):
            acc = None
            for o in range(occ):
                lhs = rows[d, p, o].reshape(2 * width, rows.shape[-1])
                rhs = cols[v, match[d][o * n_vrow + v]]
                rhs = rhs.reshape(rhs.shape[0] * rhs.shape[1], rhs.shape[2])
                t = lax.dot_general(lhs, rhs, (((1,), (1,)), ((), ())), preferred_element_type=jnp.float32)
                acc = t if acc is None else acc + t
            n = acc.shape[1]
            part[d, p, :, v * n : (v + 1) * n] = acc * scale
        s = q if d == 0 else partner(q, d, n_vcol)
        g = s * pieces + p
        dest = g // per_chunk
        place = g - dest * per_chunk
        c = pltpu.make_async_remote_copy(
            src_ref=part.at[d, p],
            dst_ref=got.at[f, place],
            send_sem=part_send.at[d, p],
            recv_sem=part_recv.at[f, place],
            device_id={"field": dest},
            device_id_type=MESH,
        )

        @pl.when(dest != f)
        def _():
            c.start()

        @pl.when(dest == f)
        def _():
            got[f, place] = part[d, p]

        part_sends.append((dest, c))

    for p in range(pieces):
        if relay:
            for p2 in (p,):
                row_copy[1, p2].wait_recv()
                to_y, to_x = {"vcol": partner(q, 2, 4)}, {"vcol": partner(q, 1, 4)}
                a = send(rows.at[1, p2, pl.ds(0, half)], rows.at[3, p2, pl.ds(0, half)],
                         row_send.at[3, p2], row_recv.at[3, p2], to_y)
                row_copy[2, p2].wait_recv()
                b = send(rows.at[2, p2, pl.ds(half, occ - half)], rows.at[3, p2, pl.ds(half, occ - half)],
                         row_send.at[0, p2], row_recv.at[0, p2], to_x)
                row_copy[3, p2] = (a, b)
        compute(0, p)
        if not relay:
            for d in range(1, n_vcol):
                row_copy[d, p].wait_recv()
                compute(d, p)
            continue
        compute(1, p)
        compute(2, p)
        if p:
            for c in row_copy[3, p - 1]:
                c.wait_recv()
            compute(3, p - 1)
    if relay:
        for c in row_copy[3, pieces - 1]:
            c.wait_recv()
        compute(3, pieces - 1)

    for place in range(per_chunk):
        for d in range(1, n_field):
            src = lax.rem(f + d, n_field)
            pltpu.make_async_remote_copy(
                src_ref=part.at[0, 0],
                dst_ref=got.at[src, place],
                send_sem=part_send.at[0, 0],
                recv_sem=part_recv.at[src, place],
                device_id={"field": src},
                device_id_type=MESH,
            ).wait_recv()
        total = got[0, place]
        for k in range(1, n_field):
            total = total + got[k, place]
        out[place] = total
    for c in sends:
        c.wait_send()
    for dest, c in part_sends:
        @pl.when(dest != f)
        def _():
            c.wait_send()


def on_device(blocks, block_ids, block_counts):
    n_field, n_vrow, n_vcol = (lax.axis_size(a) for a in ("field", "vrow", "vcol"))
    vs, occ, ch, x = blocks.shape
    chunk = n_vcol * vs // n_field
    width = min(vs // MAX_PIECES, chunk)
    pieces = vs // width
    per_chunk = chunk // width
    data = blocks.reshape(pieces, width, occ, ch, x).transpose(0, 2, 3, 1, 4)
    slots = jnp.arange(occ, dtype=jnp.int32)
    ids = jnp.where(slots < block_counts[0, 0], block_ids[0, 0], -1)
    meta = jnp.pad(ids[None, :], ((0, 0), (0, 128 - occ)))
    c = ch * vs
    wide = n_vrow * c
    dims = (n_field, n_vrow, n_vcol, pieces, occ, width, per_chunk)
    dma = pltpu.SemaphoreType.DMA
    scale = 1.0 / (n_field * SBLK * BLOCK)
    out = pl.pallas_call(
        functools.partial(kernel, dims, scale),
        out_shape=jax.ShapeDtypeStruct((per_chunk, ch * width, wide), jnp.float32),
        in_specs=[pl.BlockSpec(memory_space=pl.ANY), pl.BlockSpec(memory_space=pltpu.VMEM)],
        out_specs=pl.BlockSpec(memory_space=pltpu.VMEM),
        scratch_shapes=[
            pltpu.VMEM((n_vcol, pieces, occ, ch, width, x), jnp.bfloat16),
            pltpu.VMEM((n_vrow, occ + 1, ch, vs, x), jnp.bfloat16),
            pltpu.VMEM((n_vcol, pieces, ch * width, wide), jnp.float32),
            pltpu.VMEM((n_field, per_chunk, ch * width, wide), jnp.float32),
            pltpu.VMEM((n_vcol, 1, 128), jnp.int32),
            pltpu.VMEM((n_vrow, 1, 128), jnp.int32),
            pltpu.SMEM((n_vcol, 1, 128), jnp.int32),
            pltpu.SMEM((n_vrow, 1, 128), jnp.int32),
            dma((pieces,)),
            dma((pieces,)),
            dma((2,)),
            dma((n_vcol, pieces)),
            dma((n_vcol, pieces)),
            dma((n_vrow, pieces)),
            dma((n_vrow, pieces)),
            dma((n_vcol,)),
            dma((n_vcol,)),
            dma((n_vrow,)),
            dma((n_vrow,)),
            dma((n_vcol, pieces)),
            dma((n_field, per_chunk)),
        ],
        compiler_params=pltpu.CompilerParams(collective_id=0, has_side_effects=True),
    )(data, meta)
    out = out.reshape(per_chunk, ch, width, n_vrow, ch, vs)
    r = lax.axis_index("vrow")
    turned = jnp.concatenate([out[:, :, :, k:k+1] for k in range(n_vrow)] , axis=3) if n_vrow == 1 else (
        jnp.where(r == 0, out, jnp.roll(out, 1, axis=3)) if n_vrow == 2 else jnp.roll(out, r, axis=3)
    )
    return turned.transpose(0, 2, 1, 3, 4, 5).reshape(chunk, ch, n_vrow, 1, ch, vs)


def solution(mesh):
    placed = (
        P(("vrow", "vcol"), "field", None, None),
        P(("vrow", "vcol"), "field", None),
        P(("vrow", "vcol"), "field"),
    )
    return jax.shard_map(
        on_device,
        mesh=mesh,
        in_specs=placed,
        out_specs=P(("vrow", "field"), None, None, "vcol", None, None),
        check_vma=False,
    )
```

profile of v0, /device:TPU:6, one launch (start us, length us, event | category | flops | bytes accessed | tf_op | source)
XLA Modules:
  0.0 68.5 jit_solution(810566715015882824)
XLA Ops:
  0.0 2.2 %copy.11 = bf16[4,32,6,2,256]{4,1,3,2,0:T(8,128)(2,1)} copy(bf16[4,32,6,2,256]{4,3,2,1,0:T(2,128)(2,1)} %bitcast.12) | data formatting | bytes 1572864 | tf_op jit(solution)/shard_map/reshape | solution.py:216
  2.8 0.0 copy-start
  2.8 0.6 copy-done
  3.5 0.5 pad.4.meta
  4.0 61.5 %shard_map.37 = f32[4,64,512]{2,1,0:T(8,128)} custom-call(bf16[4,6,2,32,256]{4,3,2,1,0:T(8,128)(2,1)} %bitcast.11, s32[1,128]{1,0:T(1,128)} %pad.4.meta), custom_call_target="tpu_custom_call" | custom-call | tf_op jit(solution)/shard_map/pallas_call | solution.py:225
  65.5 1.4 %reshape.27 = f32[4,2,32,2,2,128]{5,4,3,2,1,0:T(2,128)S(1)} reshape(f32[4,64,512]{2,1,0:T(8,128)} %shard_map.37) | data formatting | bytes 1048576 | tf_op jit(solution)/shard_map/reshape | solution.py:255
  66.9 0.3 fusion.1
  67.2 0.3 fusion
  67.5 1.0 %copy.7 = f32[4,32,2,2,2,128]{5,4,3,2,1,0:T(2,128)} copy(f32[4,32,2,2,2,128]{5,4,3,1,2,0:T(2,128)S(1)} %fusion) | data formatting | bytes 1048576 | tf_op jit(solution)/shard_map/transpose | solution.py:260
  (1 shorter events, 0.0 us)
Async XLA Ops:
  2.8 0.7 copy-start
where the time goes:
time: 68.7 us; the launch traced here: 68.5 us
  Pallas kernels  61.5 us (90%)
  local copies, waits for them, and re-layouts  5.93 us (9%)
  between operations  0.69 us (1%)
    pallas_call x1, Pallas kernels, on_device(): pl.pallas_call(functools.partial(kernel, dims, scale), out_shape=jax.Shap...  61.5 us
    reshape x1, local copies, waits for them, and re-layouts, on_device(): data = blocks.reshape(pieces, width, occ, ch, x).transpose(0, 2, 3, 1, 4)  2.16 us

commit v1 on v0

--- a/solution.py
+++ b/solution.py
@@ -10,6 +10,8 @@
 SBLK = 12
 BLOCK = 256
 MAX_PIECES = 4
+LEVELS = 65535.0
+HALF = 32768
 MESH = pl.DeviceIdType.MESH
 
 
@@ -20,10 +22,10 @@
 
 
 def kernel(
-    dims, scale, data, meta, out, rows, cols, part, got, rmeta, cmeta, rids, cids,
+    dims, scale, data, meta, out, rows, cols, part, code, tops, got, got_tops, mine_sum, rmeta, cmeta, rids, cids,
     col_local, row_local, meta_local,
     row_send, row_recv, col_send, col_recv, rm_send, rm_recv, cm_send, cm_recv,
-    part_send, part_recv,
+    part_send, part_recv, top_send, top_recv,
 ):
     n_field, n_vrow, n_vcol, pieces, occ, width, per_chunk = dims
     f, r, q = lax.axis_index("field"), lax.axis_index("vrow"), lax.axis_index("vcol")
@@ -131,79 +133,91 @@
                 t = lax.dot_general(lhs, rhs, (((1,), (1,)), ((), ())), preferred_element_type=jnp.float32)
                 acc = t if acc is None else acc + t
             n = acc.shape[1]
-            part[d, p, :, v * n : (v + 1) * n] = acc * scale
+            at = pl.multiple_of(lax.rem(r + v, n_vrow) * n, n)
+            part[d, p, :, pl.ds(at, n)] = acc
+            top = jnp.max(acc, axis=0, keepdims=True)
+            inverse = jnp.where(top > 0, 1.0 / top, 0.0)
+            level = ((acc * inverse) * LEVELS + 0.5).astype(jnp.int32) - HALF
+            code[d, p, :, pl.ds(at, n)] = level.astype(jnp.int16)
+            tops[d, p, :, pl.ds(at, n)] = top
         s = q if d == 0 else partner(q, d, n_vcol)
         g = s * pieces + p
         dest = g // per_chunk
         place = g - dest * per_chunk
+        to = {"field": dest}
         c = pltpu.make_async_remote_copy(
-            src_ref=part.at[d, p],
-            dst_ref=got.at[f, place],
-            send_sem=part_send.at[d, p],
-            recv_sem=part_recv.at[f, place],
-            device_id={"field": dest},
-            device_id_type=MESH,
+            src_ref=code.at[d, p], dst_ref=got.at[f, place],
+            send_sem=part_send.at[d, p], recv_sem=part_recv.at[f, place],
+            device_id=to, device_id_type=MESH,
+        )
+        t = pltpu.make_async_remote_copy(
+            src_ref=tops.at[d, p], dst_ref=got_tops.at[f, place],
+            send_sem=top_send.at[d, p], recv_sem=top_recv.at[f, place],
+            device_id=to, device_id_type=MESH,
         )
 
         @pl.when(dest != f)
         def _():
+            t.start()
             c.start()
 
         @pl.when(dest == f)
         def _():
-            got[f, place] = part[d, p]
-
-        part_sends.append((dest, c))
+            mine_sum[place] = part[d, p]
+
+        part_sends.append((dest, c, t))
+
+    def forward(p):
+        row_copy[1, p].wait_recv()
+        a = send(rows.at[1, p, pl.ds(0, half)], rows.at[3, p, pl.ds(0, half)],
+                 row_send.at[3, p], row_recv.at[3, p], {"vcol": partner(q, 2, 4)})
+        row_copy[2, p].wait_recv()
+        b = send(rows.at[2, p, pl.ds(half, occ - half)], rows.at[3, p, pl.ds(half, occ - half)],
+                 row_send.at[0, p], row_recv.at[0, p], {"vcol": partner(q, 1, 4)})
+        row_copy[3, p] = (a, b)
 
     for p in range(pieces):
+        compute(0, p)
         if relay:
-            for p2 in (p,):
-                row_copy[1, p2].wait_recv()
-                to_y, to_x = {"vcol": partner(q, 2, 4)}, {"vcol": partner(q, 1, 4)}
-                a = send(rows.at[1, p2, pl.ds(0, half)], rows.at[3, p2, pl.ds(0, half)],
-                         row_send.at[3, p2], row_recv.at[3, p2], to_y)
-                row_copy[2, p2].wait_recv()
-                b = send(rows.at[2, p2, pl.ds(half, occ - half)], rows.at[3, p2, pl.ds(half, occ - half)],
-                         row_send.at[0, p2], row_recv.at[0, p2], to_x)
-                row_copy[3, p2] = (a, b)
-        compute(0, p)
-        if not relay:
-            for d in range(1, n_vcol):
+            forward(p)
+        for d in range(1, 3 if relay else n_vcol):
+            if not relay:
                 row_copy[d, p].wait_recv()
-                compute(d, p)
-            continue
-        compute(1, p)
-        compute(2, p)
-        if p:
-            for c in row_copy[3, p - 1]:
+            compute(d, p)
+    if relay:
+        for p in range(pieces):
+            for c in row_copy[3, p]:
                 c.wait_recv()
-            compute(3, p - 1)
-    if relay:
-        for c in row_copy[3, pieces - 1]:
-            c.wait_recv()
-        compute(3, pieces - 1)
+            compute(3, p)
 
     for place in range(per_chunk):
+        total = mine_sum[place]
         for d in range(1, n_field):
             src = lax.rem(f + d, n_field)
-            pltpu.make_async_remote_copy(
-                src_ref=part.at[0, 0],
-                dst_ref=got.at[src, place],
-                send_sem=part_send.at[0, 0],
-                recv_sem=part_recv.at[src, place],
-                device_id={"field": src},
-                device_id_type=MESH,
-            ).wait_recv()
-        total = got[0, place]
-        for k in range(1, n_field):
-            total = total + got[k, place]
-        out[place] = total
+            for buf, land, gone, came in (
+                (code, got, part_send, part_recv), (tops, got_tops, top_send, top_recv),
+            ):
+                pltpu.make_async_remote_copy(
+                    src_ref=buf.at[0, 0], dst_ref=land.at[src, place],
+                    send_sem=gone.at[0, 0], recv_sem=came.at[src, place],
+                    device_id={"field": src}, device_id_type=MESH,
+                ).wait_recv()
+            level = (got[src, place].astype(jnp.int32) + HALF).astype(jnp.float32)
+            total = total + level * (got_tops[src, place] * (1.0 / LEVELS))
+        total = total * scale
+        ch, n_r, ch2, vs = out.shape[1:]
+        for a in range(ch):
+            for k in range(n_r):
+                for b in range(ch2):
+                    c0 = (k * ch2 + b) * vs
+                    out[pl.ds(place * width, width), a, k, b, :] = total[a * width : (a + 1) * width, c0 : c0 + vs]
     for c in sends:
         c.wait_send()
-    for dest, c in part_sends:
+    for dest, c, t in part_sends:
         @pl.when(dest != f)
         def _():
             c.wait_send()
+            t.wait_send()
 
 
 def on_device(blocks, block_ids, block_counts):
@@ -224,14 +238,18 @@
     scale = 1.0 / (n_field * SBLK * BLOCK)
     out = pl.pallas_call(
         functools.partial(kernel, dims, scale),
-        out_shape=jax.ShapeDtypeStruct((per_chunk, ch * width, wide), jnp.float32),
+        out_shape=jax.ShapeDtypeStruct((chunk, ch, n_vrow, ch, vs), jnp.float32),
         in_specs=[pl.BlockSpec(memory_space=pl.ANY), pl.BlockSpec(memory_space=pltpu.VMEM)],
         out_specs=pl.BlockSpec(memory_space=pltpu.VMEM),
         scratch_shapes=[
             pltpu.VMEM((n_vcol, pieces, occ, ch, width, x), jnp.bfloat16),
             pltpu.VMEM((n_vrow, occ + 1, ch, vs, x), jnp.bfloat16),
             pltpu.VMEM((n_vcol, pieces, ch * width, wide), jnp.float32),
-            pltpu.VMEM((n_field, per_chunk, ch * width, wide), jnp.float32),
+            pltpu.VMEM((n_vcol, pieces, ch * width, wide), jnp.int16),
+            pltpu.VMEM((n_vcol, pieces, 1, wide), jnp.float32),
+            pltpu.VMEM((n_field, per_chunk, ch * width, wide), jnp.int16),
+            pltpu.VMEM((n_field, per_chunk, 1, wide), jnp.float32),
+            pltpu.VMEM((per_chunk, ch * width, wide), jnp.float32),
             pltpu.VMEM((n_vcol, 1, 128), jnp.int32),
             pltpu.VMEM((n_vrow, 1, 128), jnp.int32),
             pltpu.SMEM((n_vcol, 1, 128), jnp.int32),
@@ -249,15 +267,12 @@
             dma((n_vrow,)),
             dma((n_vcol, pieces)),
             dma((n_field, per_chunk)),
+            dma((n_vcol, pieces)),
+            dma((n_field, per_chunk)),
         ],
         compiler_params=pltpu.CompilerParams(collective_id=0, has_side_effects=True),
     )(data, meta)
-    out = out.reshape(per_chunk, ch, width, n_vrow, ch, vs)
-    r = lax.axis_index("vrow")
-    turned = jnp.concatenate([out[:, :, :, k:k+1] for k in range(n_vrow)] , axis=3) if n_vrow == 1 else (
-        jnp.where(r == 0, out, jnp.roll(out, 1, axis=3)) if n_vrow == 2 else jnp.roll(out, r, axis=3)
-    )
-    return turned.transpose(0, 2, 1, 3, 4, 5).reshape(chunk, ch, n_vrow, 1, ch, vs)
+    return out.reshape(chunk, ch, n_vrow, 1, ch, vs)
 
 
 def solution(mesh):

time: 68.7 us -> 51.8 us (0.75)
  Pallas kernels: 61.5 us -> 45.6 us
    pallas_call x1, Pallas kernels: 61.5 us -> 45.6 us  [on_device(): pl.pallas_call(functools.partial(kernel, dims, scale), out_shape=jax.Shap...]
    unnamed x2 -> x3, local copies, waits for them, and re-layouts: 0.65 us -> 2.62 us
    reshape x1 -> x0, local copies, waits for them, and re-layouts: 1.37 us -> none  [on_device(): out = out.reshape(per_chunk, ch, width, n_vrow, ch, vs)]
    transpose x1 -> x0, local copies, waits for them, and re-layouts: 0.97 us -> none  [on_device(): turned.transpose(0, 2, 1, 3, 4, 5).reshape(chunk, ch, n_vrow, 1, ch, vs)]
where the time goes in v1:
time: 51.8 us; the launch traced here: 51.6 us
  Pallas kernels  45.6 us (88%)
  local copies, waits for them, and re-layouts  5.3 us (10%)
  between operations  0.67 us (1%)
    pallas_call x1, Pallas kernels, on_device(): pl.pallas_call(functools.partial(kernel, dims, scale), out_shape=jax.Shap...  45.6 us
    unnamed x3, local copies, waits for them, and re-layouts  2.62 us
    reshape x1, local copies, waits for them, and re-layouts, on_device(): data = blocks.reshape(pieces, width, occ, ch, x).transpose(0, 2, 3, 1, 4)  2.16 us

profile of v1, /device:TPU:6, one launch (start us, length us, event | category | flops | bytes accessed | tf_op | source)
XLA Modules:
  0.0 51.6 jit_solution(1381169966266510552)
XLA Ops:
  0.7 0.0 copy-start
  0.7 0.6 %copy-done = s32[1,1,6]{2,1,0:T(1,128)S(1)} copy-done((s32[1,1,6]{2,1,0:T(1,128)S(1)}, s32[1,1,6]{2,1,0:T(1,128)}, u32[]{:S(2)}) %copy-start) | copy-done | bytes 48
  1.3 0.5 %pad.4.meta = s32[1,128]{1,0:T(1,128)} pad(s32[1,6]{1,0:T(1,128)S(1)} %compare_select_fusion, s32[]{:T(128)} %constant.1.clone.1), padding=0_0x0_122 | pad | bytes 540 | tf_op jit(solution)/shard_map/jit(_pad)/pad | solution.py:233
  1.8 2.2 %copy.11 = bf16[4,32,6,2,256]{4,1,3,2,0:T(8,128)(2,1)} copy(bf16[4,32,6,2,256]{4,3,2,1,0:T(2,128)(2,1)} %bitcast.13) | data formatting | bytes 1572864 | tf_op jit(solution)/shard_map/reshape | solution.py:230
  4.0 45.6 %shard_map.37 = f32[128,2,2,2,128]{4,3,2,1,0:T(2,128)} custom-call(bf16[4,6,2,32,256]{4,3,2,1,0:T(8,128)(2,1)} %bitcast.11, s32[1,128]{1,0:T(1,128)} %pad.4.meta), custom_call_target="tpu_custom_call" | custom-call | tf_op jit(solution)/shard_map/pallas_call | solution.py:239
  49.6 2.0 %copy.14 = f32[128,2,2,1,2,128]{5,4,3,2,1,0:T(2,128)} copy(f32[128,2,2,1,2,128]{5,4,3,2,1,0:T(2,128)} %bitcast.12) | data formatting | bytes 1048576
  (1 shorter events, 0.0 us)
Async XLA Ops:
  0.7 0.7 %copy-start = (s32[1,1,6]{2,1,0:T(1,128)S(1)}, s32[1,1,6]{2,1,0:T(1,128)}, u32[]{:S(2)}) copy-start(s32[1,1,6]{2,1,0:T(1,128)} %param.4) | copy-start | bytes 76

commit v2 on v1

--- a/solution.py
+++ b/solution.py
@@ -10,6 +10,7 @@
 SBLK = 12
 BLOCK = 256
 MAX_PIECES = 4
+AHEAD = 2
 LEVELS = 65535.0
 HALF = 32768
 MESH = pl.DeviceIdType.MESH
@@ -69,6 +70,12 @@
         return c
 
     row_meta, col_meta, row_copy, col_copy = {}, {}, {}, {}
+
+    def send_rows(p):
+        for d in range(1, 3 if relay else n_vcol):
+            to = {"vcol": partner(q, d, n_vcol)}
+            row_copy[d, p] = send(data.at[p], rows.at[d, p], row_send.at[d, p], row_recv.at[d, p], to)
+
     for d in range(1, n_vrow):
         to = {"vrow": lax.rem(r + d, n_vrow)}
         col_meta[d] = send(meta, cmeta.at[d], cm_send.at[d], cm_recv.at[d], to)
@@ -83,9 +90,8 @@
                 cols.at[d, pl.ds(0, occ), :, pl.ds(p * width, width), :],
                 col_send.at[d, p], col_recv.at[d, p], to,
             )
-        for d in range(1, 3 if relay else n_vcol):
-            to = {"vcol": partner(q, d, n_vcol)}
-            row_copy[d, p] = send(data.at[p], rows.at[d, p], row_send.at[d, p], row_recv.at[d, p], to)
+        if p < (AHEAD if relay else pieces):
+            send_rows(p)
 
     for c in local:
         c.wait()
@@ -175,20 +181,27 @@
         b = send(rows.at[2, p, pl.ds(half, occ - half)], rows.at[3, p, pl.ds(half, occ - half)],
                  row_send.at[0, p], row_recv.at[0, p], {"vcol": partner(q, 1, 4)})
         row_copy[3, p] = (a, b)
-
+        if p + AHEAD < pieces:
+            send_rows(p + AHEAD)
+
+    compute(0, 0)
     for p in range(pieces):
-        compute(0, p)
         if relay:
             forward(p)
         for d in range(1, 3 if relay else n_vcol):
             if not relay:
                 row_copy[d, p].wait_recv()
             compute(d, p)
+        if p + 1 < pieces:
+            compute(0, p + 1)
+        if relay and p:
+            for c in row_copy[3, p - 1]:
+                c.wait_recv()
+            compute(3, p - 1)
     if relay:
-        for p in range(pieces):
-            for c in row_copy[3, p]:
-                c.wait_recv()
-            compute(3, p)
+        for c in row_copy[3, pieces - 1]:
+            c.wait_recv()
+        compute(3, pieces - 1)
 
     for place in range(per_chunk):
         total = mine_sum[place]

time: 51.8 us -> 46.8 us (0.903)
  Pallas kernels: 45.6 us -> 40.6 us
    pallas_call x1, Pallas kernels: 45.6 us -> 40.6 us  [on_device(): pl.pallas_call(functools.partial(kernel, dims, scale), out_shape=jax.Shap...]
where the time goes in v2:
time: 46.8 us; the launch traced here: 46.5 us
  Pallas kernels  40.6 us (87%)
  local copies, waits for them, and re-layouts  5.3 us (11%)
  between operations  0.67 us (1%)
    pallas_call x1, Pallas kernels, on_device(): pl.pallas_call(functools.partial(kernel, dims, scale), out_shape=jax.Shap...  40.6 us
    unnamed x3, local copies, waits for them, and re-layouts  2.62 us
    reshape x1, local copies, waits for them, and re-layouts, on_device(): data = blocks.reshape(pieces, width, occ, ch, x).transpose(0, 2, 3, 1, 4)  2.16 us

profile of v2, /device:TPU:6, one launch (start us, length us, event | category | flops | bytes accessed | tf_op | source)
XLA Modules:
  0.0 46.5 jit_solution(18187443780723639958)
XLA Ops:
  0.7 0.0 copy-start
  0.7 0.6 %copy-done = s32[1,1,6]{2,1,0:T(1,128)S(1)} copy-done((s32[1,1,6]{2,1,0:T(1,128)S(1)}, s32[1,1,6]{2,1,0:T(1,128)}, u32[]{:S(2)}) %copy-start) | copy-done | bytes 48
  1.3 0.5 %pad.4.meta = s32[1,128]{1,0:T(1,128)} pad(s32[1,6]{1,0:T(1,128)S(1)} %compare_select_fusion, s32[]{:T(128)} %constant.1.clone.1), padding=0_0x0_122 | pad | bytes 540 | tf_op jit(solution)/shard_map/jit(_pad)/pad | solution.py:246
  1.8 2.2 %copy.11 = bf16[4,32,6,2,256]{4,1,3,2,0:T(8,128)(2,1)} copy(bf16[4,32,6,2,256]{4,3,2,1,0:T(2,128)(2,1)} %bitcast.13) | data formatting | bytes 1572864 | tf_op jit(solution)/shard_map/reshape | solution.py:243
  4.0 40.6 %shard_map.37 = f32[128,2,2,2,128]{4,3,2,1,0:T(2,128)} custom-call(bf16[4,6,2,32,256]{4,3,2,1,0:T(8,128)(2,1)} %bitcast.11, s32[1,128]{1,0:T(1,128)} %pad.4.meta), custom_call_target="tpu_custom_call" | custom-call | tf_op jit(solution)/shard_map/pallas_call | solution.py:252
  44.6 2.0 %copy.14 = f32[128,2,2,1,2,128]{5,4,3,2,1,0:T(2,128)} copy(f32[128,2,2,1,2,128]{5,4,3,2,1,0:T(2,128)} %bitcast.12) | data formatting | bytes 1048576
  (1 shorter events, 0.0 us)
Async XLA Ops:
  0.7 0.7 %copy-start = (s32[1,1,6]{2,1,0:T(1,128)S(1)}, s32[1,1,6]{2,1,0:T(1,128)}, u32[]{:S(2)}) copy-start(s32[1,1,6]{2,1,0:T(1,128)} %param.4) | copy-start | bytes 76

commit v3 on v2

--- a/solution.py
+++ b/solution.py
@@ -23,8 +23,8 @@
 
 
 def kernel(
-    dims, scale, data, meta, out, rows, cols, part, code, tops, got, got_tops, mine_sum, rmeta, cmeta, rids, cids,
-    col_local, row_local, meta_local,
+    dims, scale, data, meta, out, rows, raw_cols, cols, part, code, tops, got, got_tops, mine_sum, rmeta, cmeta, rids, cids,
+    row_local, meta_local,
     row_send, row_recv, col_send, col_recv, rm_send, rm_recv, cm_send, cm_recv,
     part_send, part_recv, top_send, top_recv,
 ):
@@ -40,16 +40,8 @@
     for d in range(1, n_field):
         pl.semaphore_signal(barrier, inc=1, device_id={"field": lax.rem(f + d, n_field)}, device_id_type=MESH)
 
-    local = []
-    for p in range(pieces):
-        own = pltpu.make_async_copy(
-            data.at[p], cols.at[0, pl.ds(0, occ), :, pl.ds(p * width, width), :], col_local.at[p]
-        )
-        own.start()
-        local.append(own)
-        own = pltpu.make_async_copy(data.at[p], rows.at[0, p], row_local.at[p])
-        own.start()
-        local.append(own)
+    own = pltpu.make_async_copy(data, rows.at[0], row_local.at[0])
+    own.start()
     own_r = pltpu.make_async_copy(meta, rids.at[0], meta_local.at[0])
     own_r.start()
     own_c = pltpu.make_async_copy(meta, cids.at[0], meta_local.at[1])
@@ -58,6 +50,9 @@
         cols[v, occ] = jnp.zeros_like(cols[v, occ])
 
     pl.semaphore_wait(barrier, n_vcol + n_vrow + n_field - 3)
+
+    def span(p):
+        return pl.ds(p * width, width)
 
     sends = []
 
@@ -74,7 +69,7 @@
     def send_rows(p):
         for d in range(1, 3 if relay else n_vcol):
             to = {"vcol": partner(q, d, n_vcol)}
-            row_copy[d, p] = send(data.at[p], rows.at[d, p], row_send.at[d, p], row_recv.at[d, p], to)
+            row_copy[d, p] = send(data.at[span(p)], rows.at[d, span(p)], row_send.at[d, p], row_recv.at[d, p], to)
 
     for d in range(1, n_vrow):
         to = {"vrow": lax.rem(r + d, n_vrow)}
@@ -86,15 +81,14 @@
         for d in range(1, n_vrow):
             to = {"vrow": lax.rem(r + d, n_vrow)}
             col_copy[d, p] = send(
-                data.at[p],
-                cols.at[d, pl.ds(0, occ), :, pl.ds(p * width, width), :],
+                data.at[span(p)],
+                raw_cols.at[d, span(p)],
                 col_send.at[d, p], col_recv.at[d, p], to,
             )
         if p < (AHEAD if relay else pieces):
             send_rows(p)
 
-    for c in local:
-        c.wait()
+    own.wait()
     own_r.wait()
     own_c.wait()
     for d in range(1, n_vrow):
@@ -105,8 +99,17 @@
     for d in range(1, n_vrow):
         for p in range(pieces):
             col_copy[d, p].wait_recv()
-
-    half = occ // 2
+    ch, vs = rows.shape[3], rows.shape[1]
+    n = ch * vs
+    to_row = lax.broadcasted_iota(jnp.int32, (n, n), 0)
+    from_row = lax.broadcasted_iota(jnp.int32, (n, n), 1)
+    order = jnp.where(from_row == lax.rem(to_row, vs) * ch + to_row // vs, 1.0, 0.0).astype(jnp.bfloat16)
+    for v in range(n_vrow):
+        for o in range(occ):
+            block = (raw_cols[v, :, o] if v else rows[0, :, o]).reshape(n, rows.shape[-1])
+            turned = jnp.dot(order, block, preferred_element_type=jnp.float32)
+            cols[v, o] = turned.astype(jnp.bfloat16)
+
     match = {}
     part_sends = []
 
@@ -133,9 +136,8 @@
         for v in range(n_vrow):
             acc = None
             for o in range(occ):
-                lhs = rows[d, p, o].reshape(2 * width, rows.shape[-1])
+                lhs = rows[d, p * width : (p + 1) * width, o].reshape(ch * width, rows.shape[-1])
                 rhs = cols[v, match[d][o * n_vrow + v]]
-                rhs = rhs.reshape(rhs.shape[0] * rhs.shape[1], rhs.shape[2])
                 t = lax.dot_general(lhs, rhs, (((1,), (1,)), ((), ())), preferred_element_type=jnp.float32)
                 acc = t if acc is None else acc + t
             n = acc.shape[1]
@@ -174,11 +176,13 @@
         part_sends.append((dest, c, t))
 
     def forward(p):
+        first = pl.ds(p * width, width // 2)
+        second = pl.ds(p * width + width // 2, width - width // 2)
         row_copy[1, p].wait_recv()
-        a = send(rows.at[1, p, pl.ds(0, half)], rows.at[3, p, pl.ds(0, half)],
+        a = send(rows.at[1, first], rows.at[3, first],
                  row_send.at[3, p], row_recv.at[3, p], {"vcol": partner(q, 2, 4)})
         row_copy[2, p].wait_recv()
-        b = send(rows.at[2, p, pl.ds(half, occ - half)], rows.at[3, p, pl.ds(half, occ - half)],
+        b = send(rows.at[2, second], rows.at[3, second],
                  row_send.at[0, p], row_recv.at[0, p], {"vcol": partner(q, 1, 4)})
         row_copy[3, p] = (a, b)
         if p + AHEAD < pieces:
@@ -218,12 +222,9 @@
             level = (got[src, place].astype(jnp.int32) + HALF).astype(jnp.float32)
             total = total + level * (got_tops[src, place] * (1.0 / LEVELS))
         total = total * scale
-        ch, n_r, ch2, vs = out.shape[1:]
-        for a in range(ch):
-            for k in range(n_r):
-                for b in range(ch2):
-                    c0 = (k * ch2 + b) * vs
-                    out[pl.ds(place * width, width), a, k, b, :] = total[a * width : (a + 1) * width, c0 : c0 + vs]
+        parts = n_vrow * ch
+        for k in range(parts):
+            out[pl.ds(place * ch * width * parts + k, ch * width, parts), :] = total[:, k * vs : (k + 1) * vs]
     for c in sends:
         c.wait_send()
     for dest, c, t in part_sends:
@@ -240,7 +241,7 @@
     width = min(vs // MAX_PIECES, chunk)
     pieces = vs // width
     per_chunk = chunk // width
-    data = blocks.reshape(pieces, width, occ, ch, x).transpose(0, 2, 3, 1, 4)
+    data = blocks
     slots = jnp.arange(occ, dtype=jnp.int32)
     ids = jnp.where(slots < block_counts[0, 0], block_ids[0, 0], -1)
     meta = jnp.pad(ids[None, :], ((0, 0), (0, 128 - occ)))
@@ -251,12 +252,13 @@
     scale = 1.0 / (n_field * SBLK * BLOCK)
     out = pl.pallas_call(
         functools.partial(kernel, dims, scale),
-        out_shape=jax.ShapeDtypeStruct((chunk, ch, n_vrow, ch, vs), jnp.float32),
+        out_shape=jax.ShapeDtypeStruct((chunk * ch * n_vrow * ch, vs), jnp.float32),
         in_specs=[pl.BlockSpec(memory_space=pl.ANY), pl.BlockSpec(memory_space=pltpu.VMEM)],
         out_specs=pl.BlockSpec(memory_space=pltpu.VMEM),
         scratch_shapes=[
-            pltpu.VMEM((n_vcol, pieces, occ, ch, width, x), jnp.bfloat16),
-            pltpu.VMEM((n_vrow, occ + 1, ch, vs, x), jnp.bfloat16),
+            pltpu.VMEM((n_vcol, vs, occ, ch, x), jnp.bfloat16),
+            pltpu.VMEM((n_vrow, vs, occ, ch, x), jnp.bfloat16),
+            pltpu.VMEM((n_vrow, occ + 1, ch * vs, x), jnp.bfloat16),
             pltpu.VMEM((n_vcol, pieces, ch * width, wide), jnp.float32),
             pltpu.VMEM((n_vcol, pieces, ch * width, wide), jnp.int16),
             pltpu.VMEM((n_vcol, pieces, 1, wide), jnp.float32),
@@ -267,8 +269,7 @@
             pltpu.VMEM((n_vrow, 1, 128), jnp.int32),
             pltpu.SMEM((n_vcol, 1, 128), jnp.int32),
             pltpu.SMEM((n_vrow, 1, 128), jnp.int32),
-            dma((pieces,)),
-            dma((pieces,)),
+            dma((1,)),
             dma((2,)),
             dma((n_vcol, pieces)),
             dma((n_vcol, pieces)),

time: 46.8 us -> 44.4 us (0.949)
  local copies, waits for them, and re-layouts: 5.3 us -> 3.14 us
    reshape x1 -> x0, local copies, waits for them, and re-layouts: 2.16 us -> none  [on_device(): data = blocks.reshape(pieces, width, occ, ch, x).transpose(0, 2, 3, 1, 4)]
where the time goes in v3:
time: 44.4 us; the launch traced here: 44.2 us
  Pallas kernels  40.4 us (91%)
  local copies, waits for them, and re-layouts  3.14 us (7%)
  between operations  0.67 us (2%)
    pallas_call x1, Pallas kernels, on_device(): pl.pallas_call(functools.partial(kernel, dims, scale), out_shape=jax.Shap...  40.4 us
    unnamed x3, local copies, waits for them, and re-layouts  2.62 us

profile of v3, /device:TPU:6, one launch (start us, length us, event | category | flops | bytes accessed | tf_op | source)
XLA Modules:
  0.0 44.2 jit_solution(13767847106735416289)
XLA Ops:
  0.7 0.0 copy-start
  0.7 0.6 %copy-done = s32[1,1,6]{2,1,0:T(1,128)S(1)} copy-done((s32[1,1,6]{2,1,0:T(1,128)S(1)}, s32[1,1,6]{2,1,0:T(1,128)}, u32[]{:S(2)}) %copy-start) | copy-done | bytes 48
  1.3 0.5 %pad.4.meta = s32[1,128]{1,0:T(1,128)} pad(s32[1,6]{1,0:T(1,128)S(1)} %compare_select_fusion, s32[]{:T(128)} %constant.1.clone.1), padding=0_0x0_122 | pad | bytes 540 | tf_op jit(solution)/shard_map/jit(_pad)/pad | solution.py:247
  1.8 40.4 %shard_map.37 = f32[1024,128]{1,0:T(8,128)} custom-call(bf16[128,6,2,256]{3,2,1,0:T(2,128)(2,1)} %data.1, s32[1,128]{1,0:T(1,128)} %pad.4.meta), custom_call_target="tpu_custom_call" | custom-call | tf_op jit(solution)/shard_map/pallas_call | solution.py:253
  42.3 2.0 %copy.7 = f32[128,2,2,1,2,128]{5,4,3,2,1,0:T(2,128)} copy(f32[128,2,2,1,2,128]{5,4,3,2,1,0:T(2,128)} %bitcast.7) | data formatting | bytes 1048576
  (1 shorter events, 0.0 us)
Async XLA Ops:
  0.7 0.7 %copy-start = (s32[1,1,6]{2,1,0:T(1,128)S(1)}, s32[1,1,6]{2,1,0:T(1,128)}, u32[]{:S(2)}) copy-start(s32[1,1,6]{2,1,0:T(1,128)} %param.4) | copy-start | bytes 76

commit v4 on v3

--- a/solution.py
+++ b/solution.py
@@ -23,7 +23,7 @@
 
 
 def kernel(
-    dims, scale, data, meta, out, rows, raw_cols, cols, part, code, tops, got, got_tops, mine_sum, rmeta, cmeta, rids, cids,
+    dims, scale, data, ids, counts, out, meta, rows, raw_cols, cols, part, code, tops, got, got_tops, mine_sum, rmeta, cmeta, rids, cids,
     row_local, meta_local,
     row_send, row_recv, col_send, col_recv, rm_send, rm_recv, cm_send, cm_recv,
     part_send, part_recv, top_send, top_recv,
@@ -40,16 +40,20 @@
     for d in range(1, n_field):
         pl.semaphore_signal(barrier, inc=1, device_id={"field": lax.rem(f + d, n_field)}, device_id_type=MESH)
 
+    meta[...] = jnp.full_like(meta, -1)
+    slots = lax.broadcasted_iota(jnp.int32, (1, occ), 1)
+    meta[:, 0:occ] = jnp.where(slots < counts[...], ids[0], -1)
     own = pltpu.make_async_copy(data, rows.at[0], row_local.at[0])
     own.start()
+    for v in range(n_vrow):
+        cols[v, occ] = jnp.zeros_like(cols[v, occ])
+
+    pl.semaphore_wait(barrier, n_vcol + n_vrow + n_field - 3)
+
     own_r = pltpu.make_async_copy(meta, rids.at[0], meta_local.at[0])
     own_r.start()
     own_c = pltpu.make_async_copy(meta, cids.at[0], meta_local.at[1])
     own_c.start()
-    for v in range(n_vrow):
-        cols[v, occ] = jnp.zeros_like(cols[v, occ])
-
-    pl.semaphore_wait(barrier, n_vcol + n_vrow + n_field - 3)
 
     def span(p):
         return pl.ds(p * width, width)
@@ -221,7 +225,6 @@
                 ).wait_recv()
             level = (got[src, place].astype(jnp.int32) + HALF).astype(jnp.float32)
             total = total + level * (got_tops[src, place] * (1.0 / LEVELS))
-        total = total * scale
         parts = n_vrow * ch
         for k in range(parts):
             out[pl.ds(place * ch * width * parts + k, ch * width, parts), :] = total[:, k * vs : (k + 1) * vs]
@@ -242,9 +245,6 @@
     pieces = vs // width
     per_chunk = chunk // width
     data = blocks
-    slots = jnp.arange(occ, dtype=jnp.int32)
-    ids = jnp.where(slots < block_counts[0, 0], block_ids[0, 0], -1)
-    meta = jnp.pad(ids[None, :], ((0, 0), (0, 128 - occ)))
     c = ch * vs
     wide = n_vrow * c
     dims = (n_field, n_vrow, n_vcol, pieces, occ, width, per_chunk)
@@ -253,9 +253,10 @@
     out = pl.pallas_call(
         functools.partial(kernel, dims, scale),
         out_shape=jax.ShapeDtypeStruct((chunk * ch * n_vrow * ch, vs), jnp.float32),
-        in_specs=[pl.BlockSpec(memory_space=pl.ANY), pl.BlockSpec(memory_space=pltpu.VMEM)],
+        in_specs=[pl.BlockSpec(memory_space=pl.ANY)] + [pl.BlockSpec(memory_space=pltpu.VMEM)] * 2,
         out_specs=pl.BlockSpec(memory_space=pltpu.VMEM),
         scratch_shapes=[
+            pltpu.VMEM((1, 128), jnp.int32),
             pltpu.VMEM((n_vcol, vs, occ, ch, x), jnp.bfloat16),
             pltpu.VMEM((n_vrow, vs, occ, ch, x), jnp.bfloat16),
             pltpu.VMEM((n_vrow, occ + 1, ch * vs, x), jnp.bfloat16),
@@ -285,8 +286,8 @@
             dma((n_field, per_chunk)),
         ],
         compiler_params=pltpu.CompilerParams(collective_id=0, has_side_effects=True),
-    )(data, meta)
-    return out.reshape(chunk, ch, n_vrow, 1, ch, vs)
+    )(data, block_ids, block_counts)
+    return (out * scale).reshape(chunk, ch, n_vrow, 1, ch, vs)
 
 
 def solution(mesh):

time: 44.4 us -> 43.2 us (0.973)
  local copies, waits for them, and re-layouts: 3.14 us -> 0 us
  other arithmetic: 0.01 us -> 1.88 us
    unnamed x3 -> x0, local copies, waits for them, and re-layouts: 2.62 us -> none
    mul x0 -> x1, other arithmetic: none -> 1.88 us  [on_device(): return (out * scale).reshape(chunk, ch, n_vrow, 1, ch, vs)]
    pad x1 -> x0, local copies, waits for them, and re-layouts: 0.52 us -> none  [on_device(): meta = jnp.pad(ids[None, :], ((0, 0), (0, 128 - occ)))]
where the time goes in v4:
time: 43.2 us; the launch traced here: 43 us
  Pallas kernels  40.5 us (94%)
  other arithmetic  1.88 us (4%)
  between operations  0.66 us (2%)
    pallas_call x1, Pallas kernels, on_device(): pl.pallas_call(functools.partial(kernel, dims, scale), out_shape=jax.Shap...  40.5 us
    mul x1, other arithmetic, on_device(): return (out * scale).reshape(chunk, ch, n_vrow, 1, ch, vs)  1.88 us

profile of v4, /device:TPU:6, one launch (start us, length us, event | category | flops | bytes accessed | tf_op | source)
XLA Modules:
  0.0 43.0 jit_solution(8540415538800455788)
XLA Ops:
  0.7 40.5 %shard_map.37 = f32[1024,128]{1,0:T(8,128)} custom-call(bf16[128,6,2,256]{3,2,1,0:T(2,128)(2,1)} %data.1, s32[1,1,6]{2,1,0:T(1,128)} %ids.1, s32[1,1]{1,0:T(1,128)S(6)} %copy.5.counts), custom_call_target="tpu_custom_call" | custom-call | tf_op jit(solution)/shard_map/pallas_call | solution.py:253
  41.1 1.9 %broadcast_multiply_fusion = f32[1024,128]{1,0:T(8,128)} fusion(f32[1024,128]{1,0:T(8,128)} %shard_map.37), kind=kLoop, calls=%fused_computation | loop fusion | flops 131072 | bytes 1048576 | tf_op jit(solution)/shard_map/mul | solution.py:290
